TPU v7x, 32 devices: a whole 2x2x4 slice. The times are simulated.
32 devices in a mesh: fiber: 8 (over z, core), group: 4 (over y, x).
Axes of the slice: x: 2, y: 2, z: 4, core: 2. Of those that a mesh axis runs over, the one named last changes fastest.
Arguments:
- field_slab: float32 [512, 64, 2048], P('fiber', 'group'), may hold values from -42 to 42
- start_basis: float32 [512, 128], replicated, may hold values from -6 to 6
Outputs:
- factor: float32 [512, 128], replicated
- core_slab: float32 [128, 64, 2048], P(None, 'group', 'fiber')
All inputs are finite; a program needn't handle non-finite values.
Results may differ from a plain program's by a relative error of at most 0.0003.
Values sent between devices are 32-bit elements; how exact they have to be, the bound alone decides.
No kernel may reach another device: no remote copies, remote signals or barrier semaphores. Data moves between devices by JAX's collectives and lax.ppermute only.
A program may use at most 128 MiB of HBM per device.

v0:
```python
import jax
import jax.numpy as jnp
from jax import lax
from jax.sharding import PartitionSpec as P

ITERS = 2
precise = lax.Precision.HIGHEST


def orthonormal(images):
    inner_products = jnp.dot(images.T, images, precision=precise)
    cholesky_factor = jnp.linalg.cholesky(inner_products)
    return lax.linalg.triangular_solve(
        cholesky_factor, images, left_side=False, lower=True, transpose_a=True
    )


def on_device(field_slab, start_basis):
    column_count = field_slab.shape[1] * field_slab.shape[2] * lax.axis_size("group")
    regrouped = lax.all_to_all(field_slab, "fiber", split_axis=2, concat_axis=0, tiled=True)
    columns = regrouped.reshape(regrouped.shape[0], regrouped.shape[1] * regrouped.shape[2])
    local_gram = jnp.dot(columns, columns.T, precision=precise)
    subspace = start_basis
    fiber_share = lax.psum_scatter(local_gram, "fiber", scatter_dimension=0, tiled=True)
    gram_share = lax.psum(fiber_share, "group") / column_count
    for iteration in range(ITERS):
        image_rows = jnp.dot(gram_share, subspace, precision=precise)
        subspace = orthonormal(lax.all_gather(image_rows, "fiber", axis=0, tiled=True))
    core_slab = jnp.einsum("mk,mbc->kbc", subspace, regrouped, precision=precise)
    return (subspace, core_slab)


def solution(mesh):
    return jax.shard_map(
        on_device,
        mesh=mesh,
        in_specs=(P("fiber", "group", None), P()),
        out_specs=(P(), P(None, "group", "fiber")),
        check_vma=False,
    )
```

profile of v0, /device:TPU:0, one launch (start us, length us, event | category | flops | bytes accessed | tf_op | source)
XLA Modules:
  0.0 485.6 jit_solution(11098625435497381214)
XLA Ops:
  7.2 0.0 copy-start
  7.2 0.0 reduce-scatter.2.cloned.1.call-start
  7.2 15.6 %copy.22 = f32[64,16,2048]{0,1,2:T(8,128)} copy(f32[64,16,2048]{2,1,0:T(8,128)} %param.5) | data formatting | bytes 16777216 | tf_op args[0]
  22.8 15.4 %reshape.27 = f32[8,1,262144]{2,1,0:T(1,128)} reshape(f32[2048,16,64]{2,1,0:T(8,128)} %bitcast.49) | data formatting | bytes 16777216
  38.2 190.7 %all_to_all.18 = f32[8,1,262144]{2,1,0:T(1,128)} all-to-all(f32[8,1,262144]{2,1,0:T(1,128)} %reshape.27), channel_id=1, replica_groups=mesh['fiber'=8,'group'=4] {'fiber'}, dimensions={0} | all-to-all | bytes 16777216 | tf_op jit(solution)/shard_map/all_to_all | solution.py:20
  228.9 0.5 broadcast.36
  229.4 26.2 %reduce.4 = f32[8,262144]{1,0:T(8,128)} reduce(f32[8,1,262144]{2,1,0:T(1,128)} %all_to_all.18, f32[]{:T(128)} %broadcast.36), dimensions={1}, to_apply=%all_to_all.13.reduce_sub_computation | reduce | bytes 16777220 | tf_op jit(solution)/shard_map/all_to_all | solution.py:20
  255.7 15.6 %reshape.28 = f32[2048,16,64]{2,1,0:T(8,128)} reshape(f32[8,262144]{1,0:T(8,128)} %reduce.4) | data formatting | bytes 16777216
  271.3 15.8 %copy.23 = f32[64,16,8,256]{3,1,0,2:T(8,128)} copy(f32[64,16,8,256]{0,1,3,2:T(8,128)} %bitcast.47) | data formatting | bytes 16777216 | tf_op jit(solution)/shard_map/all_to_all | solution.py:20
  287.0 11.5 %copy.30 = f32[64,8,16,256]{3,1,2,0:T(8,128)S(1)} copy(f32[64,8,16,256]{3,2,1,0:T(8,128)} %bitcast.51) | data formatting | bytes 16777216
  298.5 14.9 %fusion.19 = f32[512,512]{1,0:T(8,128)} fusion(f32[512,4096]{1,0:T(8,128)S(1)} %bitcast.46), kind=kOutput, calls=%fused_computation.29 | convolution fusion | flops 12884901888 | bytes 9437184 | tf_op jit(solution)/shard_map/dot_general | solution.py:22
  313.5 0.0 reduce-scatter.2.cloned.1.call-update
  313.5 0.0 all-reduce.2.cloned.1.call-start
  313.5 32.2 %reduce-scatter.2.cloned.1.call-done = f32[64,512]{1,0:T(8,128)} async-done(((f32[512,512]{1,0:T(8,128)}), f32[64,512]{1,0:T(8,128)}) %reduce-scatter.2.cloned.1.call-update) | async-done | bytes 131088 | tf_op jit(solution)/shard_map/reduce_scatter | solution.py:24
  345.7 0.0 all-reduce.2.cloned.1.call-update
  345.7 12.8 %copy.26 = f32[8,64,16,256]{3,1,0,2:T(8,128)} copy(f32[8,64,16,256]{1,2,3,0:T(8,128)} %bitcast.48) | data formatting | bytes 16777216 | tf_op jit(solution)/shard_map/all_to_all | solution.py:20
  358.5 30.5 %all-reduce.2.cloned.1.call-done = f32[64,512]{1,0:T(8,128)} async-done(((f32[64,512]{1,0:T(8,128)}), f32[64,512]{1,0:T(8,128)}) %all-reduce.2.cloned.1.call-update) | async-done | bytes 131088 | tf_op jit(solution)/shard_map/psum | solution.py:25
  389.0 0.0 copy-done
  389.0 1.2 fusion.4
  390.2 14.3 %all_gather.6 = f32[512,128]{1,0:T(8,128)S(1)} all-gather(f32[64,128]{1,0:T(8,128)S(1)} %fusion.4), channel_id=1, replica_groups=mesh['fiber'=8,'group'=4] {'fiber'}, dimensions={0}, use_global_device_ids=true | all-gather | bytes 294912 | tf_op jit(solution)/shard_map/all_gather | solution.py:28
  404.5 0.6 fusion.20
  405.1 0.1 copy.24
  405.2 11.7 %cholesky.44 = f32[128,128]{1,0:T(8,128)S(1)} custom-call(f32[128,128]{1,0:T(8,128)S(1)} %fusion.12), custom_call_target="Cholesky" | custom-call | tf_op jit(solution)/shard_map/jit(cholesky)/cholesky | solution.py:12
  416.9 0.6 compare_reduce_fusion.1
  417.6 0.7 fusion.6
  418.2 9.8 %custom-call.6 = f32[1,128,128]{1,2,0:T(8,128)S(1)} custom-call(f32[1,128,128]{2,1,0:T(8,128)S(1)} %fusion.6), custom_call_target="InvertDiagBlocksLowerTriangular" | custom-call | tf_op jit(solution)/shard_map/triangular_solve/custom-call.0 | solution.py:13
  428.0 0.4 convolution_bitcast_fusion
  428.5 1.3 fusion.2
  429.8 14.4 %all_gather.7 = f32[512,128]{1,0:T(8,128)S(1)} all-gather(f32[64,128]{1,0:T(8,128)S(1)} %fusion.2), channel_id=1, replica_groups=mesh['fiber'=8,'group'=4] {'fiber'}, dimensions={0}, use_global_device_ids=true | all-gather | bytes 294912 | tf_op jit(solution)/shard_map/all_gather | solution.py:28
  444.2 0.6 fusion.21
  444.8 0.1 copy.25
  444.9 11.7 %cholesky.55 = f32[128,128]{1,0:T(8,128)S(1)} custom-call(f32[128,128]{1,0:T(8,128)S(1)} %fusion.10), custom_call_target="Cholesky" | custom-call | tf_op jit(solution)/shard_map/jit(cholesky)/cholesky | solution.py:12
  456.7 0.6 compare_reduce_fusion
  457.3 0.7 fusion.7
  458.0 9.8 %custom-call.7 = f32[1,128,128]{1,2,0:T(8,128)S(1)} custom-call(f32[1,128,128]{2,1,0:T(8,128)S(1)} %fusion.7), custom_call_target="InvertDiagBlocksLowerTriangular" | custom-call | tf_op jit(solution)/shard_map/triangular_solve/custom-call.0 | solution.py:13
  467.8 0.4 fusion.8
  468.2 0.8 copy.27
  469.1 6.9 %fusion = f32[128,16,256]{2,0,1:T(8,128)S(1)} fusion(f32[512,16,256]{2,0,1:T(8,128)} %bitcast.50, f32[128,512]{1,0:T(8,128)S(1)} %fusion.8), kind=kOutput, calls=%fused_computation.1 | convolution fusion | flops 3221225472 | bytes 10747904 | tf_op jit(solution)/shard_map/mk,mbc->kbc/dot_general | solution.py:29
  476.0 2.5 copy.28
  (4 shorter events, 0.1 us)
Async XLA Ops:
  7.2 381.9 %copy-start = (f32[512,128]{1,0:T(8,128)S(1)}, f32[512,128]{1,0:T(8,128)}, u32[]{:S(2)}) copy-start(f32[512,128]{1,0:T(8,128)} %param.6) | copy-start | bytes 786436
  7.2 338.5 %reduce-scatter.2.cloned.1.call-start = ((), (), s32[]{:S(2)}) async-start(), calls=%async_computation.2 | async-start | bytes 1179648 | tf_op jit(solution)/shard_map/reduce_scatter | solution.py:24
  313.5 75.5 %all-reduce.2.cloned.1.call-start = ((), (), s32[]{:S(2)}) async-start(), calls=%async_computation.3 | async-start | bytes 262144 | tf_op jit(solution)/shard_map/psum | solution.py:25
Sparse Core Ops, SparseCore 0:
  313.6 32.0 reduce-scatter.1
  348.6 40.4 all-reduce.1
where the time goes:
time: 489 us; the launch traced here: 486 us
  blocking collectives  219 us (45%)
  local copies, waits for them, and re-layouts  90.7 us (19%)
  other arithmetic  72 us (15%)
  waiting for transfers between devices  62.7 us (13%)
  matrix products  26.3 us (5%)
  between operations  14.4 us (3%)
    all_to_all x1, blocking collectives, on_device(): lax.all_to_all(field_slab, 'fiber', split_axis=2, concat_axis=0, tiled=True)  191 us
    unnamed x8, local copies, waits for them, and re-layouts  61.4 us
    reduce_scatter x1, waiting for transfers between devices, on_device(): lax.psum_scatter(local_gram, 'fiber', scatter_dimension=0, tiled=True)  32.2 us
    psum x1, waiting for transfers between devices, on_device(): gram_share = lax.psum(fiber_share, 'group') / column_count  30.5 us
    all_to_all x3, local copies, waits for them, and re-layouts, on_device(): lax.all_to_all(field_slab, 'fiber', split_axis=2, concat_axis=0, tiled=True)  29.1 us
    all_gather x2, blocking collectives, on_device(): lax.all_gather(image_rows, 'fiber', axis=0, tiled=True)  28.7 us
    all_to_all x1, other arithmetic, on_device(): lax.all_to_all(field_slab, 'fiber', split_axis=2, concat_axis=0, tiled=True)  26.2 us
    another operation x6, other arithmetic, orthonormal(): cholesky_factor = jnp.linalg.cholesky(inner_products)  24.8 us
  transfers between devices with their start and end apart: 2, of which 2 were waited for; matrix products, arithmetic and copies ran while one was open for 3% of the time, Pallas kernels for 0%

commit v1 on v0

--- a/solution.py
+++ b/solution.py
@@ -5,6 +5,28 @@
 
 ITERS = 2
 precise = lax.Precision.HIGHEST
+
+
+def laid_out(blocks, dim):
+    blocks = jnp.moveaxis(blocks, 0, dim)
+    shape = blocks.shape
+    return blocks.reshape(*shape[:dim], shape[dim] * shape[dim + 1], *shape[dim + 2 :])
+
+
+def ring_gather(x, axis, dim):
+    size = lax.axis_size(axis)
+    pairs = [(i, (i + 1) % size) for i in range(size)]
+    back = [(b, a) for a, b in pairs]
+    lower, upper = ([], [])
+    for hop in range(size - 1):
+        if hop % 2 == 0:
+            lower.append(lax.ppermute(lower[-1] if lower else x, axis, pairs))
+        else:
+            upper.append(lax.ppermute(upper[-1] if upper else x, axis, back))
+    tiles = jnp.stack([*lower[::-1], x, *upper])
+    shift = lax.axis_index(axis) - len(lower)
+    tiles = tiles[(jnp.arange(size) - shift) % size]
+    return laid_out(tiles, dim)
 
 
 def orthonormal(images):
@@ -25,7 +47,7 @@
     gram_share = lax.psum(fiber_share, "group") / column_count
     for iteration in range(ITERS):
         image_rows = jnp.dot(gram_share, subspace, precision=precise)
-        subspace = orthonormal(lax.all_gather(image_rows, "fiber", axis=0, tiled=True))
+        subspace = orthonormal(ring_gather(image_rows, "fiber", 0))
     core_slab = jnp.einsum("mk,mbc->kbc", subspace, regrouped, precision=precise)
     return (subspace, core_slab)
 

time: 489 us -> 516 us (1.055)
  waiting for transfers between devices: 62.7 us -> 95.6 us
  blocking collectives: 219 us -> 191 us
  starting transfers between devices: 0.08 us -> 22 us
    all_gather x2 -> x0, blocking collectives: 28.7 us -> none  [on_device(): lax.all_gather(image_rows, 'fiber', axis=0, tiled=True)]
    ppermute x0 -> x14, starting transfers between devices: none -> 21.9 us  [the longest x6 21.8 us: ring_gather(): upper.append(lax.ppermute(upper[-1] if upper else x, axis, back))]
    ppermute x0 -> x14, waiting for transfers between devices: none -> 20.1 us  [the longest x8 18.3 us: ring_gather(): lower.append(lax.ppermute(lower[-1] if lower else x, axis, pairs))]
    psum x1, waiting for transfers between devices: 30.5 us -> 43.3 us  [on_device(): gram_share = lax.psum(fiber_share, 'group') / column_count]
    unnamed x8 -> x22, local copies, waits for them, and re-layouts: 61.4 us -> 61.5 us
  transfers between devices with their start and end apart: 2 -> 16, of which waited for: 2 -> 11; matrix products, arithmetic and copies ran while one was open for 3% -> 3% of each run, Pallas kernels for 0% -> 0%
where the time goes in v1:
time: 516 us; the launch traced here: 513 us
  blocking collectives  191 us (37%)
  waiting for transfers between devices  95.6 us (19%)
  local copies, waits for them, and re-layouts  91.5 us (18%)
  other arithmetic  72 us (14%)
  matrix products  26.2 us (5%)
  starting transfers between devices  22 us (4%)
  between operations  14.6 us (3%)
    all_to_all x1, blocking collectives, on_device(): lax.all_to_all(field_slab, 'fiber', split_axis=2, concat_axis=0, tiled=True)  191 us
    unnamed x22, local copies, waits for them, and re-layouts  61.5 us
    psum x1, waiting for transfers between devices, on_device(): gram_share = lax.psum(fiber_share, 'group') / column_count  43.3 us
    reduce_scatter x1, waiting for transfers between devices, on_device(): lax.psum_scatter(local_gram, 'fiber', scatter_dimension=0, tiled=True)  32.3 us
    all_to_all x3, local copies, waits for them, and re-layouts, on_device(): lax.all_to_all(field_slab, 'fiber', split_axis=2, concat_axis=0, tiled=True)  28.7 us
    all_to_all x1, other arithmetic, on_device(): lax.all_to_all(field_slab, 'fiber', split_axis=2, concat_axis=0, tiled=True)  26.2 us
    another operation x6, other arithmetic, orthonormal(): cholesky_factor = jnp.linalg.cholesky(inner_products)  24.8 us
    ppermute x6, starting transfers between devices, ring_gather(): upper.append(lax.ppermute(upper[-1] if upper else x, axis, back))  21.8 us
  transfers between devices with their start and end apart: 16, of which 11 were waited for; matrix products, arithmetic and copies ran while one was open for 3% of the time, Pallas kernels for 0%

profile of v1, /device:TPU:0, one launch (start us, length us, event | category | flops | bytes accessed | tf_op | source)
XLA Modules:
  0.0 512.8 jit_solution(7434897409822934454)
XLA Ops:
  7.2 15.5 %copy.22 = f32[64,16,2048]{0,1,2:T(8,128)} copy(f32[64,16,2048]{2,1,0:T(8,128)} %param.5) | data formatting | bytes 16777216 | tf_op args[0]
  22.8 15.4 %reshape.102 = f32[8,1,262144]{2,1,0:T(1,128)} reshape(f32[2048,16,64]{2,1,0:T(8,128)} %bitcast.89) | data formatting | bytes 16777216
  38.2 190.9 %all_to_all.18 = f32[8,1,262144]{2,1,0:T(1,128)} all-to-all(f32[8,1,262144]{2,1,0:T(1,128)} %reshape.102), channel_id=1, replica_groups=mesh['fiber'=8,'group'=4] {'fiber'}, dimensions={0} | all-to-all | bytes 16777216 | tf_op jit(solution)/shard_map/all_to_all | solution.py:42
  229.1 0.5 broadcast.108
  229.6 26.2 %reduce.4 = f32[8,262144]{1,0:T(8,128)} reduce(f32[8,1,262144]{2,1,0:T(1,128)} %all_to_all.18, f32[]{:T(128)} %broadcast.108), dimensions={1}, to_apply=%all_to_all.13.reduce_sub_computation | reduce | bytes 16777220 | tf_op jit(solution)/shard_map/all_to_all | solution.py:42
  255.8 15.6 %reshape.103 = f32[2048,16,64]{2,1,0:T(8,128)} reshape(f32[8,262144]{1,0:T(8,128)} %reduce.4) | data formatting | bytes 16777216
  271.5 15.4 %copy.23 = f32[64,16,8,256]{3,1,0,2:T(8,128)} copy(f32[64,16,8,256]{0,1,3,2:T(8,128)} %bitcast.87) | data formatting | bytes 16777216 | tf_op jit(solution)/shard_map/all_to_all | solution.py:42
  286.9 11.5 %copy.30 = f32[64,8,16,256]{3,1,2,0:T(8,128)S(1)} copy(f32[64,8,16,256]{3,2,1,0:T(8,128)} %bitcast.91) | data formatting | bytes 16777216
  298.4 14.7 %fusion.21 = f32[512,512]{1,0:T(8,128)} fusion(f32[512,4096]{1,0:T(8,128)S(1)} %bitcast.86), kind=kOutput, calls=%fused_computation.56 | convolution fusion | flops 12884901888 | bytes 9437184 | tf_op jit(solution)/shard_map/dot_general | solution.py:44
  313.2 32.3 %reduce-scatter.2.cloned.1.call-done = f32[64,512]{1,0:T(8,128)} async-done(((f32[512,512]{1,0:T(8,128)}), f32[64,512]{1,0:T(8,128)}) %reduce-scatter.2.cloned.1.call-update) | async-done | bytes 131088 | tf_op jit(solution)/shard_map/reduce_scatter | solution.py:46
  345.5 43.3 %all-reduce.2.cloned.1.call-done = f32[64,512]{1,0:T(8,128)} async-done(((f32[64,512]{1,0:T(8,128)}), f32[64,512]{1,0:T(8,128)}) %all-reduce.2.cloned.1.call-update) | async-done | bytes 131088 | tf_op jit(solution)/shard_map/psum | solution.py:47
  388.8 1.2 fusion.4
  390.0 5.1 collective-permute-done
  395.1 3.5 collective-permute-start.4
  398.7 1.9 collective-permute-done.1
  400.6 3.6 collective-permute-start.5
  404.2 1.6 collective-permute-done.2
  405.8 3.8 collective-permute-start.6
  409.6 1.3 collective-permute-done.3
  411.0 0.2 collective-permute-done.6
  411.2 0.6 gather_fusion
  411.8 0.6 convolution_bitcast_fusion.2
  412.4 0.1 copy.24
  412.5 11.7 %cholesky.44 = f32[128,128]{1,0:T(8,128)S(1)} custom-call(f32[128,128]{1,0:T(8,128)S(1)} %fusion.12), custom_call_target="Cholesky" | custom-call | tf_op jit(solution)/shard_map/jit(cholesky)/cholesky | solution.py:34
  424.2 0.6 compare_reduce_fusion.1
  424.9 0.7 fusion.6
  425.5 9.8 %custom-call.6 = f32[1,128,128]{1,2,0:T(8,128)S(1)} custom-call(f32[1,128,128]{2,1,0:T(8,128)S(1)} %fusion.6), custom_call_target="InvertDiagBlocksLowerTriangular" | custom-call | tf_op jit(solution)/shard_map/triangular_solve/custom-call.0 | solution.py:35
  435.3 0.4 convolution_bitcast_fusion
  435.8 1.3 fusion.2
  437.1 5.1 collective-permute-done.7
  442.3 3.5 collective-permute-start.11
  445.8 1.7 collective-permute-done.8
  447.5 3.5 collective-permute-start.12
  451.0 1.6 collective-permute-done.9
  452.6 12.7 %copy.26 = f32[8,64,16,256]{3,1,0,2:T(8,128)} copy(f32[8,64,16,256]{1,2,3,0:T(8,128)} %bitcast.88) | data formatting | bytes 16777216 | tf_op jit(solution)/shard_map/all_to_all | solution.py:42
  465.4 3.8 collective-permute-start.13
  469.2 1.5 collective-permute-done.13
  470.8 0.6 gather_fusion.1
  471.3 0.6 convolution_bitcast_fusion.1
  471.9 0.1 copy.25
  472.0 11.7 %cholesky.55 = f32[128,128]{1,0:T(8,128)S(1)} custom-call(f32[128,128]{1,0:T(8,128)S(1)} %fusion.10), custom_call_target="Cholesky" | custom-call | tf_op jit(solution)/shard_map/jit(cholesky)/cholesky | solution.py:34
  483.8 0.6 compare_reduce_fusion
  484.4 0.7 fusion.7
  485.1 9.8 %custom-call.7 = f32[1,128,128]{1,2,0:T(8,128)S(1)} custom-call(f32[1,128,128]{2,1,0:T(8,128)S(1)} %fusion.7), custom_call_target="InvertDiagBlocksLowerTriangular" | custom-call | tf_op jit(solution)/shard_map/triangular_solve/custom-call.0 | solution.py:35
  494.9 0.4 fusion.8
  495.3 6.9 %fusion = f32[128,16,256]{2,0,1:T(8,128)S(1)} fusion(f32[512,16,256]{2,0,1:T(8,128)} %bitcast.90, f32[128,512]{1,0:T(8,128)S(1)} %fusion.8), kind=kOutput, calls=%fused_computation.5 | convolution fusion | flops 3221225472 | bytes 10747904 | tf_op jit(solution)/shard_map/mk,mbc->kbc/dot_general | solution.py:51
  502.3 2.5 copy.28
  504.8 0.8 copy.27
  (41 shorter events, 0.5 us)
Async XLA Ops:
  7.2 381.6 %copy-start = (f32[512,128]{1,0:T(8,128)S(1)}, f32[512,128]{1,0:T(8,128)}, u32[]{:S(2)}) copy-start(f32[512,128]{1,0:T(8,128)} %param.6) | copy-start | bytes 786436
  7.2 338.3 %reduce-scatter.2.cloned.1.call-start = ((), (), s32[]{:S(2)}) async-start(), calls=%async_computation.2 | async-start | bytes 1179648 | tf_op jit(solution)/shard_map/reduce_scatter | solution.py:46
  313.2 75.6 %all-reduce.2.cloned.1.call-start = ((), (), s32[]{:S(2)}) async-start(), calls=%async_computation.3 | async-start | bytes 262144 | tf_op jit(solution)/shard_map/psum | solution.py:47
  389.9 5.2 %collective-permute-start = (f32[64,128]{1,0:T(8,128)S(1)}, f32[64,128]{1,0:T(8,128)S(1)}, u32[]{:S(2)}, u32[]{:S(2)}) collective-permute-start(f32[64,128]{1,0:T(8,128)S(1)} %fusion.4), channel_id=1, source_target_pairs={{0,4},{4,8},{8,12},{12,16},{16,20},{20,24},{24,28},{28,0},{1,5},{5... | collective-permute-start | bytes 98312 | tf_op jit(solution)/shard_map/ppermute | solution.py:23
  395.1 5.5 %collective-permute-start.1 = (f32[64,128]{1,0:T(8,128)S(1)}, f32[64,128]{1,0:T(8,128)S(1)}, u32[]{:S(2)}, u32[]{:S(2)}) collective-permute-start(f32[64,128]{1,0:T(8,128)S(1)} %collective-permute-done), channel_id=1, source_target_pairs={{0,4},{4,8},{8,12},{12,16},{16,20},{20,24},{24,28},{28,0},{1,5},{5... | collective-permute-start | bytes 98312 | tf_op jit(solution)/shard_map/ppermute | solution.py:23
  395.1 5.5 %collective-permute-start.4 = (f32[64,128]{1,0:T(8,128)S(1)}, f32[64,128]{1,0:T(8,128)S(1)}, u32[]{:S(2)}, u32[]{:S(2)}) collective-permute-start(f32[64,128]{1,0:T(8,128)S(1)} %fusion.4), channel_id=1, source_target_pairs={{4,0},{8,4},{12,8},{16,12},{20,16},{24,20},{28,24},{0,28},{5,1},{9... | collective-permute-start | bytes 98312 | tf_op jit(solution)/shard_map/ppermute | solution.py:25
  400.6 5.2 %collective-permute-start.2 = (f32[64,128]{1,0:T(8,128)S(1)}, f32[64,128]{1,0:T(8,128)S(1)}, u32[]{:S(2)}, u32[]{:S(2)}) collective-permute-start(f32[64,128]{1,0:T(8,128)S(1)} %collective-permute-done.1), channel_id=1, source_target_pairs={{0,4},{4,8},{8,12},{12,16},{16,20},{20,24},{24,28},{28,0},{1,5},{5... | collective-permute-start | bytes 98312 | tf_op jit(solution)/shard_map/ppermute | solution.py:23
  400.6 5.2 %collective-permute-start.5 = (f32[64,128]{1,0:T(8,128)S(1)}, f32[64,128]{1,0:T(8,128)S(1)}, u32[]{:S(2)}, u32[]{:S(2)}) collective-permute-start(f32[64,128]{1,0:T(8,128)S(1)} %collective-permute-done.4), channel_id=1, source_target_pairs={{4,0},{8,4},{12,8},{16,12},{20,16},{24,20},{28,24},{0,28},{5,1},{9... | collective-permute-start | bytes 98312 | tf_op jit(solution)/shard_map/ppermute | solution.py:25
  405.8 5.1 %collective-permute-start.3 = (f32[64,128]{1,0:T(8,128)S(1)}, f32[64,128]{1,0:T(8,128)S(1)}, u32[]{:S(2)}, u32[]{:S(2)}) collective-permute-start(f32[64,128]{1,0:T(8,128)S(1)} %collective-permute-done.2), channel_id=1, source_target_pairs={{0,4},{4,8},{8,12},{12,16},{16,20},{20,24},{24,28},{28,0},{1,5},{5... | collective-permute-start | bytes 98312 | tf_op jit(solution)/shard_map/ppermute | solution.py:23
  405.8 5.4 %collective-permute-start.6 = (f32[64,128]{1,0:T(8,128)S(1)}, f32[64,128]{1,0:T(8,128)S(1)}, u32[]{:S(2)}, u32[]{:S(2)}) collective-permute-start(f32[64,128]{1,0:T(8,128)S(1)} %collective-permute-done.5), channel_id=1, source_target_pairs={{4,0},{8,4},{12,8},{16,12},{20,16},{24,20},{28,24},{0,28},{5,1},{9... | collective-permute-start | bytes 98312 | tf_op jit(solution)/shard_map/ppermute | solution.py:25
  437.1 5.2 %collective-permute-start.7 = (f32[64,128]{1,0:T(8,128)S(1)}, f32[64,128]{1,0:T(8,128)S(1)}, u32[]{:S(2)}, u32[]{:S(2)}) collective-permute-start(f32[64,128]{1,0:T(8,128)S(1)} %fusion.2), channel_id=1, source_target_pairs={{0,4},{4,8},{8,12},{12,16},{16,20},{20,24},{24,28},{28,0},{1,5},{5... | collective-permute-start | bytes 98312 | tf_op jit(solution)/shard_map/ppermute | solution.py:23
  442.3 5.2 %collective-permute-start.8 = (f32[64,128]{1,0:T(8,128)S(1)}, f32[64,128]{1,0:T(8,128)S(1)}, u32[]{:S(2)}, u32[]{:S(2)}) collective-permute-start(f32[64,128]{1,0:T(8,128)S(1)} %collective-permute-done.7), channel_id=1, source_target_pairs={{0,4},{4,8},{8,12},{12,16},{16,20},{20,24},{24,28},{28,0},{1,5},{5... | collective-permute-start | bytes 98312 | tf_op jit(solution)/shard_map/ppermute | solution.py:23
  442.3 5.2 %collective-permute-start.11 = (f32[64,128]{1,0:T(8,128)S(1)}, f32[64,128]{1,0:T(8,128)S(1)}, u32[]{:S(2)}, u32[]{:S(2)}) collective-permute-start(f32[64,128]{1,0:T(8,128)S(1)} %fusion.2), channel_id=1, source_target_pairs={{4,0},{8,4},{12,8},{16,12},{20,16},{24,20},{28,24},{0,28},{5,1},{9... | collective-permute-start | bytes 98312 | tf_op jit(solution)/shard_map/ppermute | solution.py:25
  447.5 5.1 %collective-permute-start.9 = (f32[64,128]{1,0:T(8,128)S(1)}, f32[64,128]{1,0:T(8,128)S(1)}, u32[]{:S(2)}, u32[]{:S(2)}) collective-permute-start(f32[64,128]{1,0:T(8,128)S(1)} %collective-permute-done.8), channel_id=1, source_target_pairs={{0,4},{4,8},{8,12},{12,16},{16,20},{20,24},{24,28},{28,0},{1,5},{5... | collective-permute-start | bytes 98312 | tf_op jit(solution)/shard_map/ppermute | solution.py:23
  447.5 17.9 %collective-permute-start.12 = (f32[64,128]{1,0:T(8,128)S(1)}, f32[64,128]{1,0:T(8,128)S(1)}, u32[]{:S(2)}, u32[]{:S(2)}) collective-permute-start(f32[64,128]{1,0:T(8,128)S(1)} %collective-permute-done.11), channel_id=1, source_target_pairs={{4,0},{8,4},{12,8},{16,12},{20,16},{24,20},{28,24},{0,28},{5,1},{9... | collective-permute-start | bytes 98312 | tf_op jit(solution)/shard_map/ppermute | solution.py:25
  452.6 16.5 %collective-permute-start.10 = (f32[64,128]{1,0:T(8,128)S(1)}, f32[64,128]{1,0:T(8,128)S(1)}, u32[]{:S(2)}, u32[]{:S(2)}) collective-permute-start(f32[64,128]{1,0:T(8,128)S(1)} %collective-permute-done.9), channel_id=1, source_target_pairs={{0,4},{4,8},{8,12},{12,16},{16,20},{20,24},{24,28},{28,0},{1,5},{5... | collective-permute-start | bytes 98312 | tf_op jit(solution)/shard_map/ppermute | solution.py:23
  465.4 5.4 %collective-permute-start.13 = (f32[64,128]{1,0:T(8,128)S(1)}, f32[64,128]{1,0:T(8,128)S(1)}, u32[]{:S(2)}, u32[]{:S(2)}) collective-permute-start(f32[64,128]{1,0:T(8,128)S(1)} %collective-permute-done.12), channel_id=1, source_target_pairs={{4,0},{8,4},{12,8},{16,12},{20,16},{24,20},{28,24},{0,28},{5,1},{9... | collective-permute-start | bytes 98312 | tf_op jit(solution)/shard_map/ppermute | solution.py:25
Sparse Core Ops, SparseCore 0:
  313.3 32.1 reduce-scatter.1
  348.3 40.3 all-reduce.1
